TPU v7x, 32 devices: a whole 2x2x4 slice. The times are simulated.
32 devices in a mesh: cell: 8 (over z, y), region: 4 (over x, core).
Axes of the slice: x: 2, y: 2, z: 4, core: 2. Of those that a mesh axis runs over, the one named last changes fastest.
Arguments:
- observed: bfloat16 [8192, 16384], P('cell', 'region'), may hold values from -0.5 to 0.5
- block_mask: int32 [1024, 128], P('cell', 'region'), may hold values 0 or 1
- plan: int32 [4], replicated, may hold values from 0 to 3, each once
- cell_factors: float32 [8192, 256], P('cell'), may hold values from -6 to 6
- region_factors: float32 [32768, 256], P(('cell', 'region')), may hold values from -6 to 6
Outputs:
- new_cells: float32 [8192, 256], P('cell')
- new_regions: float32 [32768, 256], P(('cell', 'region'))
Inputs may be any that keep to these rules, and one draw needn't show every extreme that they name: `plan`: each stored slot 0 to 3 appears once.
All inputs are finite; a program needn't handle non-finite values. No bound on the sum of `block_mask` on one device may be relied on, other than what follows from the above.
Results may differ from a plain program's by a relative error of at most 0.0056.
Values sent between devices are 32-bit elements; how exact they have to be, the bound alone decides.
No kernel may reach another device: no remote copies, remote signals or barrier semaphores. Data moves between devices by JAX's collectives and lax.ppermute only.
A program may use at most 64 MiB of HBM per device.

v0:
```python
import math

import jax
import jax.numpy as jnp
from jax import lax
from jax.sharding import PartitionSpec as P

STRATA = 4


beta_mom = 0.9


def shifted(value, axis, steps):
    count = lax.axis_size(axis)
    pairs = [(source, (source + steps) % count) for source in range(count)]
    return lax.ppermute(value, axis, pairs)


def body(observed, block_mask, plan, cell_factors, region_factors):
    n_region = lax.axis_size("region")
    cell_rows = cell_factors.shape[0]
    block_rows = region_factors.shape[0]
    total_cols = n_region * block_rows
    scale_pred = 0.5 / math.sqrt(total_cols)
    rate_region = total_cols / cell_rows
    cells_now = cell_factors
    regions_now = region_factors
    momentum = jnp.zeros_like(cell_factors)
    for section in range(STRATA):
        slot_index = plan[section]
        data_block = lax.dynamic_slice_in_dim(observed, slot_index * block_rows, block_rows, 1)
        mask_block = lax.dynamic_slice_in_dim(
            block_mask, slot_index * (block_rows // 128), block_rows // 128, 1
        )
        expanded = jnp.broadcast_to(
            mask_block[:, None, :, None], (cell_rows // 8, 8, block_rows // 128, 128)
        )
        expanded = expanded.reshape(cell_rows, block_rows).astype(jnp.float32)
        cell_bf = cells_now.astype(jnp.bfloat16)
        region_bf = regions_now.astype(jnp.bfloat16)
        predicted = lax.dot_general(
            cell_bf, region_bf, (((1,), (1,)), ((), ())), preferred_element_type=jnp.float32
        )
        resid = (expanded * (scale_pred * predicted - data_block.astype(jnp.float32))).astype(
            jnp.bfloat16
        )
        grad_cell = scale_pred * jnp.dot(resid, region_bf, preferred_element_type=jnp.float32)
        grad_region = scale_pred * lax.dot_general(
            resid, cell_bf, (((0,), (0,)), ((), ())), preferred_element_type=jnp.float32
        )
        regions_now = regions_now - rate_region * grad_region
        grad_total = lax.psum(grad_cell, "region")
        momentum = beta_mom * momentum + grad_total
        cells_now = cells_now - momentum
        if section + 1 < STRATA:
            regions_now = shifted(regions_now, "cell", -1)
    regions_now = shifted(regions_now, "cell", STRATA - 1)
    return (cells_now, regions_now)


def solution(mesh):
    in_specs = (
        P("cell", "region"),
        P("cell", "region"),
        P(),
        P("cell", None),
        P(("cell", "region"), None),
    )
    out_specs = (P("cell", None), P(("cell", "region"), None))
    return jax.shard_map(body, mesh=mesh, in_specs=in_specs, out_specs=out_specs, check_vma=False)
```

profile of v0, /device:TPU:0, one launch (start us, length us, event | category | flops | bytes accessed | tf_op | source)
XLA Modules:
  0.0 219.6 jit_solution(5115374856449592697)
XLA Ops:
  7.2 0.0 all-reduce.5.cloned.1.call-start
  7.2 1.5 fusion.26
  12.0 0.7 dynamic-slice_convert_fusion
  12.7 0.1 copy.7
  12.8 0.0 copy-start.1
  12.8 0.0 copy-start.2
  12.8 3.2 %fusion.3 = bf16[1024,1024]{1,0:T(8,128)(2,1)S(1)} fusion(bf16[1024,4096]{1,0:T(8,128)(2,1)} %param.5, s32[]{:T(128)S(6)} %select_n.25, f32[128,8]{1,0:T(8,128)S(1)} %copy.7, f32[1024,256]{1,0:T(8,128)} %param.9, f32[1024,256]{1,0:T(8,128)} %param.8), kind=kOutput, calls=%fused_computation.7 | convolution fusion | flops 542638080 | bytes 6295556 | tf_op jit(solution)/shard_map/dot_general | solution.py:42
  16.0 0.0 copy-done.1
  16.0 0.0 copy-done.2
  16.0 1.7 fusion.7
  17.8 6.0 %collective-permute-start = (f32[1024,256]{1,0:T(8,128)}, f32[1024,256]{1,0:T(8,128)S(1)}, u32[]{:S(2)}, u32[]{:S(2)}) collective-permute-start(f32[1024,256]{1,0:T(8,128)} %fusion.7), channel_id=1, source_target_pairs={{0,28},{4,0},{8,4},{12,8},{16,12},{20,16},{24,20},{28,24},{1,29},{... | collective-permute-start | bytes 3145736 | tf_op jit(solution)/shard_map/ppermute | solution.py:17
  23.8 1.7 convolution_multiply_fusion.7
  25.5 0.0 all-reduce.5.cloned.1.call-update
  25.5 0.0 all-reduce.7.cloned.1.call-start
  26.2 0.1 copy.8
  26.3 32.9 %all-reduce.5.cloned.1.call-done = f32[1024,256]{1,0:T(8,128)} async-done(((f32[1024,256]{1,0:T(8,128)}), f32[1024,256]{1,0:T(8,128)}) %all-reduce.5.cloned.1.call-update) | async-done | bytes 1048592 | tf_op jit(solution)/shard_map/psum | solution.py:53
  59.2 1.4 sub.37
  60.5 0.0 collective-permute-done
  60.6 3.3 %fusion.2 = bf16[1024,1024]{1,0:T(8,128)(2,1)S(1)} fusion(bf16[1024,4096]{1,0:T(8,128)(2,1)} %param.5, s32[]{:T(128)S(6)} %select_n.27, f32[128,8]{1,0:T(8,128)S(1)} %copy.8, f32[1024,256]{1,0:T(8,128)S(1)} %collective-permute-done, f32[1024,256]{1,0:T(8,128)S(1)} %sub.37), kind=kOutput, calls=%fused_computation.5 | convolution fusion | flops 542638080 | bytes 6295556 | tf_op jit(solution)/shard_map/dot_general | solution.py:42
  63.8 1.8 fusion.6
  65.6 0.0 copy-start
  65.6 4.2 %collective-permute-start.1 = (f32[1024,256]{1,0:T(8,128)}, f32[1024,256]{1,0:T(8,128)}, u32[]{:S(2)}, u32[]{:S(2)}) collective-permute-start(f32[1024,256]{1,0:T(8,128)} %fusion.6), channel_id=1, source_target_pairs={{0,28},{4,0},{8,4},{12,8},{16,12},{20,16},{24,20},{28,24},{1,29},{... | collective-permute-start | bytes 3145736 | tf_op jit(solution)/shard_map/ppermute | solution.py:17
  69.8 1.7 convolution_multiply_fusion.5
  71.5 0.0 all-reduce.7.cloned.1.call-update
  71.5 0.0 all-reduce.9.cloned.1.call-start
  72.3 0.1 copy.9
  72.4 32.4 %all-reduce.7.cloned.1.call-done = f32[1024,256]{1,0:T(8,128)} async-done(((f32[1024,256]{1,0:T(8,128)}), f32[1024,256]{1,0:T(8,128)}) %all-reduce.7.cloned.1.call-update) | async-done | bytes 1048592 | tf_op jit(solution)/shard_map/psum | solution.py:53
  104.8 0.0 copy-done
  104.8 1.4 fusion.8
  106.2 0.0 collective-permute-done.1
  106.2 3.6 %fusion.1 = bf16[1024,1024]{1,0:T(8,128)(2,1)S(1)} fusion(bf16[1024,4096]{1,0:T(8,128)(2,1)} %param.5, s32[]{:T(128)S(6)} %select_n.29, f32[128,8]{1,0:T(8,128)S(1)} %copy.9, f32[1024,256]{1,0:T(8,128)} %collective-permute-done.1, f32[1024,256]{1,0:T(8,128)S(1)} %fusion.8), kind=kOutput, calls=%fused_computation.3 | convolution fusion | flops 542638080 | bytes 6295556 | tf_op jit(solution)/shard_map/dot_general | solution.py:42
  109.8 3.0 %fusion.5 = f32[1024,256]{1,0:T(8,128)} fusion(f32[1024,256]{1,0:T(8,128)} %collective-permute-done.1, bf16[1024,1024]{1,0:T(8,128)(2,1)S(1)} %fusion.1, f32[1024,256]{1,0:T(8,128)S(1)} %fusion.8), kind=kOutput, calls=%fused_computation.12 | convolution fusion | flops 537657344 | bytes 5242880 | tf_op jit(solution)/shard_map/dot_general | solution.py:49
  112.8 4.2 %collective-permute-start.2 = (f32[1024,256]{1,0:T(8,128)}, f32[1024,256]{1,0:T(8,128)}, u32[]{:S(2)}, u32[]{:S(2)}) collective-permute-start(f32[1024,256]{1,0:T(8,128)} %fusion.5), channel_id=1, source_target_pairs={{0,28},{4,0},{8,4},{12,8},{16,12},{20,16},{24,20},{28,24},{1,29},{... | collective-permute-start | bytes 3145736 | tf_op jit(solution)/shard_map/ppermute | solution.py:17
  117.0 2.9 %convolution_multiply_fusion.3 = f32[1024,256]{1,0:T(8,128)} fusion(bf16[1024,1024]{1,0:T(8,128)(2,1)S(1)} %fusion.1, f32[1024,256]{1,0:T(8,128)} %collective-permute-done.1), kind=kOutput, calls=%fused_computation.13 | convolution fusion | flops 537395200 | bytes 4194304 | tf_op jit(solution)/shard_map/dot_general | solution.py:48
  119.9 0.0 all-reduce.9.cloned.1.call-update
  120.0 0.0 all-reduce.11.cloned.1.call-start
  120.7 0.1 copy.10
  120.8 32.4 %all-reduce.9.cloned.1.call-done = f32[1024,256]{1,0:T(8,128)} async-done(((f32[1024,256]{1,0:T(8,128)}), f32[1024,256]{1,0:T(8,128)}) %all-reduce.9.cloned.1.call-update) | async-done | bytes 1048592 | tf_op jit(solution)/shard_map/psum | solution.py:53
  153.2 1.8 fusion.25
  155.0 0.0 collective-permute-done.2
  155.0 3.6 %fusion = bf16[1024,1024]{1,0:T(8,128)(2,1)S(1)} fusion(bf16[1024,4096]{1,0:T(8,128)(2,1)} %param.5, s32[]{:T(128)S(6)} %select_n.31, f32[128,8]{1,0:T(8,128)S(1)} %copy.10, f32[1024,256]{1,0:T(8,128)} %collective-permute-done.2, f32[1024,256]{1,0:T(8,128)S(1)} %fusion.25), kind=kOutput, calls=%fused_computation.1 | convolution fusion | flops 542638080 | bytes 6295556 | tf_op jit(solution)/shard_map/dot_general | solution.py:42
  158.6 3.0 %fusion.4 = f32[1024,256]{1,0:T(8,128)} fusion(f32[1024,256]{1,0:T(8,128)} %collective-permute-done.2, bf16[1024,1024]{1,0:T(8,128)(2,1)S(1)} %fusion, f32[1024,256]{1,0:T(8,128)S(1)} %fusion.25), kind=kOutput, calls=%fused_computation.9 | convolution fusion | flops 537657344 | bytes 5242880 | tf_op jit(solution)/shard_map/dot_general | solution.py:49
  161.6 0.0 copy-start.3
  161.6 2.4 %collective-permute-start.3 = (f32[1024,256]{1,0:T(8,128)}, f32[1024,256]{1,0:T(8,128)}, u32[]{:S(2)}, u32[]{:S(2)}) collective-permute-start(f32[1024,256]{1,0:T(8,128)} %fusion.4), channel_id=1, source_target_pairs={{0,12},{4,16},{8,20},{12,24},{16,28},{20,0},{24,4},{28,8},{1,13},{... | collective-permute-start | bytes 3145736 | tf_op jit(solution)/shard_map/ppermute | solution.py:17
  164.0 2.9 %convolution_multiply_fusion.1 = f32[1024,256]{1,0:T(8,128)} fusion(bf16[1024,1024]{1,0:T(8,128)(2,1)S(1)} %fusion, f32[1024,256]{1,0:T(8,128)} %collective-permute-done.2), kind=kOutput, calls=%fused_computation.10 | convolution fusion | flops 537395200 | bytes 4194304 | tf_op jit(solution)/shard_map/dot_general | solution.py:48
  166.9 0.0 all-reduce.11.cloned.1.call-update
  167.0 35.3 %all-reduce.11.cloned.1.call-done = f32[1024,256]{1,0:T(8,128)} async-done(((f32[1024,256]{1,0:T(8,128)}), f32[1024,256]{1,0:T(8,128)}) %all-reduce.11.cloned.1.call-update) | async-done | bytes 1048592 | tf_op jit(solution)/shard_map/psum | solution.py:53
  202.3 0.0 copy-done.3
  202.3 2.8 %add_subtract_fusion = f32[1024,256]{1,0:T(8,128)} fusion(f32[1024,256]{1,0:T(8,128)S(1)} %fusion.25, f32[1024,256]{1,0:T(8,128)} %all-reduce.11.cloned.1.call-done, f32[1024,256]{1,0:T(8,128)} %all-reduce.9.cloned.1.call-done, f32[1024,256]{1,0:T(8,128)S(1)} %copy-done.3, f32[1024,256]{1,0:T(8,128)S(1)} %copy-done), kind=kLoop, calls=%fused_computation.20 | loop fusion | flops 1835008 | bytes 6291456 | tf_op jit(solution)/shard_map/sub | solution.py:55
  205.1 5.6 %collective-permute-done.3 = f32[1024,256]{1,0:T(8,128)} collective-permute-done((f32[1024,256]{1,0:T(8,128)}, f32[1024,256]{1,0:T(8,128)}, u32[]{:S(2)}, u32[]{:S(2)}) %collective-permute-start.3) | collective-permute-done | bytes 1048608 | tf_op jit(solution)/shard_map/ppermute | solution.py:17
  210.8 2.3 %copy.16 = f32[1024,256]{1,0:T(8,128)} copy(f32[1024,256]{1,0:T(8,128)} %collective-permute-done.3) | data formatting | bytes 2097152
Async XLA Ops:
  7.2 52.0 %all-reduce.5.cloned.1.call-start = ((), (), s32[]{:S(2)}) async-start(), calls=%async_computation | async-start | bytes 2097152 | tf_op jit(solution)/shard_map/psum | solution.py:53
  12.8 3.2 %copy-start.1 = (f32[1024,256]{1,0:T(8,128)S(1)}, f32[1024,256]{1,0:T(8,128)}, u32[]{:S(2)}) copy-start(f32[1024,256]{1,0:T(8,128)} %param.9) | copy-start | bytes 3145732
  12.8 3.2 %copy-start.2 = (f32[1024,256]{1,0:T(8,128)S(1)}, f32[1024,256]{1,0:T(8,128)}, u32[]{:S(2)}) copy-start(f32[1024,256]{1,0:T(8,128)} %param.8) | copy-start | bytes 3145732
  17.8 42.8 %collective-permute-start = (f32[1024,256]{1,0:T(8,128)}, f32[1024,256]{1,0:T(8,128)S(1)}, u32[]{:S(2)}, u32[]{:S(2)}) collective-permute-start(f32[1024,256]{1,0:T(8,128)} %fusion.7), channel_id=1, source_target_pairs={{0,28},{4,0},{8,4},{12,8},{16,12},{20,16},{24,20},{28,24},{1,29},{... | collective-permute-start | bytes 3145736 | tf_op jit(solution)/shard_map/ppermute | solution.py:17
  25.5 79.2 %all-reduce.7.cloned.1.call-start = ((), (), s32[]{:S(2)}) async-start(), calls=%async_computation.1 | async-start | bytes 2097152 | tf_op jit(solution)/shard_map/psum | solution.py:53
  65.6 39.2 %copy-start = (f32[1024,256]{1,0:T(8,128)S(1)}, f32[1024,256]{1,0:T(8,128)}, u32[]{:S(2)}) copy-start(f32[1024,256]{1,0:T(8,128)} %all-reduce.5.cloned.1.call-done) | copy-start | bytes 3145732
  65.6 40.6 %collective-permute-start.1 = (f32[1024,256]{1,0:T(8,128)}, f32[1024,256]{1,0:T(8,128)}, u32[]{:S(2)}, u32[]{:S(2)}) collective-permute-start(f32[1024,256]{1,0:T(8,128)} %fusion.6), channel_id=1, source_target_pairs={{0,28},{4,0},{8,4},{12,8},{16,12},{20,16},{24,20},{28,24},{1,29},{... | collective-permute-start | bytes 3145736 | tf_op jit(solution)/shard_map/ppermute | solution.py:17
  71.5 81.6 %all-reduce.9.cloned.1.call-start = ((), (), s32[]{:S(2)}) async-start(), calls=%async_computation.2 | async-start | bytes 2097152 | tf_op jit(solution)/shard_map/psum | solution.py:53
  112.8 42.2 %collective-permute-start.2 = (f32[1024,256]{1,0:T(8,128)}, f32[1024,256]{1,0:T(8,128)}, u32[]{:S(2)}, u32[]{:S(2)}) collective-permute-start(f32[1024,256]{1,0:T(8,128)} %fusion.5), channel_id=1, source_target_pairs={{0,28},{4,0},{8,4},{12,8},{16,12},{20,16},{24,20},{28,24},{1,29},{... | collective-permute-start | bytes 3145736 | tf_op jit(solution)/shard_map/ppermute | solution.py:17
  120.0 82.3 %all-reduce.11.cloned.1.call-start = ((), (), s32[]{:S(2)}) async-start(), calls=%async_computation.3 | async-start | bytes 2097152 | tf_op jit(solution)/shard_map/psum | solution.py:53
  161.6 40.7 %copy-start.3 = (f32[1024,256]{1,0:T(8,128)S(1)}, f32[1024,256]{1,0:T(8,128)}, u32[]{:S(2)}) copy-start(f32[1024,256]{1,0:T(8,128)} %all-reduce.7.cloned.1.call-done) | copy-start | bytes 3145732
  161.6 49.1 %collective-permute-start.3 = (f32[1024,256]{1,0:T(8,128)}, f32[1024,256]{1,0:T(8,128)}, u32[]{:S(2)}, u32[]{:S(2)}) collective-permute-start(f32[1024,256]{1,0:T(8,128)} %fusion.4), channel_id=1, source_target_pairs={{0,12},{4,16},{8,20},{12,24},{16,28},{20,0},{24,4},{28,8},{1,13},{... | collective-permute-start | bytes 3145736 | tf_op jit(solution)/shard_map/ppermute | solution.py:17
Sparse Core Ops, SparseCore 0:
  25.7 33.4 all-reduce.4
  71.7 33.0 all-reduce.6
  120.1 33.0 all-reduce.8
  167.1 35.1 all-reduce.10
where the time goes:
time: 220 us
  waiting for transfers between devices  139 us (63%)
  matrix products  32.3 us (15%)
  between operations  19.2 us (9%)
  starting transfers between devices  17.1 us (8%)
  other arithmetic  8.19 us (4%)
  local copies, waits for them, and re-layouts  4.15 us (2%)
    psum x4, waiting for transfers between devices, body(): grad_total = lax.psum(grad_cell, 'region')  133 us
    ppermute x4, starting transfers between devices, shifted(): return lax.ppermute(value, axis, pairs)  16.9 us
    dot_general x4, matrix products, body(): lax.dot_general(cell_bf, region_bf, (((1,), (1,)), ((), ())), preferred_e...  13.6 us
    dot_general x4, matrix products, body(): lax.dot_general(resid, cell_bf, (((0,), (0,)), ((), ())), preferred_eleme...  9.47 us
    dot_general x4, matrix products, body(): jnp.dot(resid, region_bf, preferred_element_type=jnp.float32)  9.23 us
    sub x4, other arithmetic, body(): cells_now = cells_now - momentum  7.45 us
    ppermute x4, waiting for transfers between devices, shifted(): return lax.ppermute(value, axis, pairs)  5.62 us
  transfers between devices with their start and end apart: 8, of which 5 were waited for; matrix products, arithmetic and copies ran while one was open for 8% of the time, Pallas kernels for 0%

commit v1 on v0

v1 whole, which is shorter than its diff:
```python
import functools
import math

import jax
import jax.numpy as jnp
from jax import lax
from jax.experimental import pallas as pl
from jax.experimental.pallas import tpu as pltpu
from jax.sharding import PartitionSpec as P


STRATA = 4
CHUNKS = 2
LANES = 128
MASK_ROWS = 8


beta_mom = 0.9


def permuted(value, axis, to):
    count = lax.axis_size(axis)
    pairs = [(source, to(source) % count) for source in range(count)]
    return lax.ppermute(value, axis, pairs)


def nt_dot(a, b):
    return lax.dot_general(a, b, (((1,), (1,)), ((), ())), preferred_element_type=jnp.float32)


def tn_dot(a, b):
    return lax.dot_general(a, b, (((0,), (0,)), ((), ())), preferred_element_type=jnp.float32)


def block_kernel(cfg, plan, observed, mask, *refs):
    section, chunk, scale, rate = cfg
    opening, first, last = section == 0, chunk == 0, chunk == CHUNKS - 1
    refs = list(refs)

    def take(count):
        got = refs[:count]
        del refs[:count]
        return got

    if first and opening:
        (cells_hbm,) = take(1)
    elif first:
        cells_ref, mom_mine, mom_other = take(3)
    else:
        cells_bf, grad_in = take(2)
    (region_ref,) = take(1)
    (new_region,) = take(1)
    if first and not opening:
        (new_cells,) = take(1)
    if first:
        (cells_bf,) = take(1)
    grads = take(2 if last else 1)
    data, wide, resid, sems = take(4)
    side = lax.axis_index("region") % 2
    slot = plan[section]
    cell_rows, m = data.shape
    half = cell_rows // 2
    tile = min(256, half)
    tiles = cell_rows // tile
    columns = mask.shape[1] // STRATA

    def fetch(source, target, at):
        copy = pltpu.make_async_copy(source, target, sems.at[at])
        copy.start()
        return copy

    if opening:
        region_buf = refs.pop(0)
        region_copy = fetch(region_ref.at[pl.ds(chunk * m, m), :], region_buf, tiles)
        if first:
            cells_buf = refs.pop(0)
            cells_copy = fetch(cells_hbm, cells_buf, tiles + 1)
        region_ref = region_buf
    start = pl.multiple_of(slot * (m * CHUNKS) + chunk * m, LANES)
    copies = [
        fetch(
            observed.at[pl.ds(i * tile, tile), pl.ds(start, m)],
            data.at[pl.ds(i * tile, tile), :],
            i,
        )
        for i in range(tiles)
    ]
    wanted = slot * columns + chunk * (m // LANES) + lax.broadcasted_iota(
        jnp.int32, (mask.shape[1], m), 1
    ) // LANES
    pick = wanted == lax.broadcasted_iota(jnp.int32, (mask.shape[1], m), 0)
    wide[...] = jnp.dot(
        mask[...].astype(jnp.bfloat16),
        pick.astype(jnp.float32).astype(jnp.bfloat16),
        preferred_element_type=jnp.float32,
    )
    if first and opening:
        cells_copy.wait()
        cells_bf[...] = cells_buf[...].astype(jnp.bfloat16)
    elif first:
        for who, mom in ((1 - side, mom_other), (side, mom_mine)):
            rows = pl.ds(pl.multiple_of(who * half, half), half)
            now = cells_ref[rows, :] - mom[...]
            new_cells[rows, :] = now
            cells_bf[rows, :] = now.astype(jnp.bfloat16)
    if opening:
        region_copy.wait()
    region_bf = region_ref[...].astype(jnp.bfloat16)
    for i in range(tiles):
        predicted = nt_dot(cells_bf[i * tile : (i + 1) * tile, :], region_bf)
        copies[i].wait()
        step = 2 * MASK_ROWS
        for r in range(0, tile, step):
            at = i * tile + r
            w = [
                jnp.broadcast_to(wide[(at + d) // MASK_ROWS : (at + d) // MASK_ROWS + 1, :], (MASK_ROWS, m))
                for d in range(0, step, MASK_ROWS)
            ]
            w = jnp.concatenate(w, 0)
            value = scale * predicted[r : r + step, :] - data[at : at + step, :].astype(jnp.float32)
            resid[at : at + step, :] = (w * value).astype(jnp.bfloat16)
    for i in range(tiles):
        per_half = tiles // 2
        if last:
            who = (1 - side) if i < per_half else side
            rows = pl.ds(pl.multiple_of(who * half + (i % per_half) * tile, tile), tile)
            target = grads[i // per_half].at[pl.ds((i % per_half) * tile, tile), :]
        else:
            rows = pl.ds(i * tile, tile)
            target = grads[0].at[rows, :]
        grad = scale * jnp.dot(resid[rows, :], region_bf, preferred_element_type=jnp.float32)
        if not first:
            grad = grad + grad_in[rows, :]
        target[...] = grad
    hsum = tn_dot(resid[...], cells_bf[...])
    new_region[...] = region_ref[...] - rate * (scale * hsum)


def block_call(section, chunk, scale, rate, plan, observed, mask, ins, region):
    opening, first, last = section == 0, chunk == 0, chunk == CHUNKS - 1
    rank = region.shape[1]
    m = region.shape[0] // CHUNKS if opening else region.shape[0]
    cell_rows = observed.shape[0]
    f32, bf16 = jnp.float32, jnp.bfloat16
    vm = pl.BlockSpec(memory_space=pltpu.VMEM)
    hbm = pl.BlockSpec(memory_space=pltpu.HBM)
    whole = (cell_rows, rank)
    outs = [jax.ShapeDtypeStruct((m, rank), f32)]
    if first and not opening:
        outs += [jax.ShapeDtypeStruct(whole, f32)]
    if first:
        outs += [jax.ShapeDtypeStruct(whole, bf16)]
    if last:
        outs += [jax.ShapeDtypeStruct((cell_rows // 2, rank), f32)] * 2
    else:
        outs += [jax.ShapeDtypeStruct(whole, f32)]
    scratch = [
        pltpu.VMEM((cell_rows, m), observed.dtype),
        pltpu.VMEM((mask.shape[0], m), f32),
        pltpu.VMEM((cell_rows, m), bf16),
        pltpu.SemaphoreType.DMA((16,)),
    ]
    if opening:
        scratch.append(pltpu.VMEM((m, rank), f32))
        if first:
            scratch.append(pltpu.VMEM(whole, f32))
    args = (plan, observed, mask, *ins, region)
    return pl.pallas_call(
        functools.partial(block_kernel, (section, chunk, scale, rate)),
        out_shape=outs,
        in_specs=[pl.BlockSpec(memory_space=pltpu.SMEM), hbm, vm]
        + [hbm if opening and first else vm] * len(ins)
        + [hbm if opening else vm],
        out_specs=[vm] * len(outs),
        scratch_shapes=scratch,
        compiler_params=pltpu.CompilerParams(vmem_limit_bytes=54 << 20),
        cost_estimate=pl.CostEstimate(
            flops=6 * cell_rows * m * rank, bytes_accessed=4 << 20, transcendentals=0
        ),
    )(*args)


def summed(value, bits, index, tag):
    bit = bits[0]
    if len(bits) == 1:
        return value + permuted(value, "region", lambda i: i ^ bit)
    side = (index // bit) % 2
    rows = value.shape[0] // 2
    mine = lax.dynamic_slice_in_dim(value, side * rows, rows, 0)
    send = lax.dynamic_slice_in_dim(value, (1 - side) * rows, rows, 0)
    mine = mine + permuted(send, "region", lambda i: i ^ bit)
    mine = summed(mine, bits[1:], index, tag)
    other = permuted(mine, "region", lambda i: i ^ bit)
    return jnp.concatenate(
        [jnp.where(side == 0, mine, other), jnp.where(side == 0, other, mine)], 0
    )


def returned(chunks):
    steps = STRATA - 1
    count = lax.axis_size("cell")
    odd = lax.axis_index("cell") % 2 == 1
    rows = chunks[0].shape[0]
    part = rows * len(chunks) // 4
    relay = permuted(chunks[0][:part], "cell", lambda i: i - 1 if i % 2 else i + steps)
    outs = []
    for k, chunk in enumerate(chunks):
        piece = chunk[part:] if k == 0 else chunk
        if piece.shape[0]:
            outs.append(permuted(piece, "cell", lambda i: i + steps))
    final = lax.ppermute(relay, "cell", [(i, (i + steps + 1) % count) for i in range(0, count, 2)])
    return jnp.concatenate([jnp.where(odd, relay, final)] + outs, 0)


def body(observed, block_mask, plan, cell_factors, region_factors):
    n_region = lax.axis_size("region")
    index = lax.axis_index("region")
    bits = [1 << p for p in range(n_region.bit_length() - 1)]
    side = index % 2
    cell_rows, _ = cell_factors.shape
    block_rows = region_factors.shape[0]
    total_cols = n_region * block_rows
    scale = 0.5 / math.sqrt(total_cols)
    rate = total_cols / cell_rows
    cells_now = cell_factors
    chunks = [region_factors] * CHUNKS
    mom_mine = mom_other = None
    for s in range(STRATA):
        grad = None
        sent = []
        for k in range(CHUNKS):
            if k == 0:
                ins = (cells_now,) if s == 0 else (cells_now, mom_mine, mom_other)
            else:
                ins = (cells_bf, grad)
            outs = block_call(s, k, scale, rate, plan, observed, block_mask, ins, chunks[k])
            new_chunk, outs = outs[0], outs[1:]
            if k == 0 and s > 0:
                cells_now, outs = outs[0], outs[1:]
            if k == 0:
                cells_bf, outs = outs[0], outs[1:]
            if k == CHUNKS - 1:
                grad_send, grad_keep = outs
            else:
                (grad,) = outs
            if s + 1 < STRATA:
                new_chunk = permuted(new_chunk, "cell", lambda i: i - 1)
            sent.append(new_chunk)
        chunks = sent
        grad_mine = grad_keep + permuted(grad_send, "region", lambda i: i ^ bits[0])
        grad_mine = summed(grad_mine, bits[1:], index, s)
        mom_mine = grad_mine if s == 0 else beta_mom * mom_mine + grad_mine
        mom_other = permuted(mom_mine, "region", lambda i: i ^ bits[0])
    regions = returned(chunks)
    mom = jnp.concatenate(
        [jnp.where(side == 0, mom_mine, mom_other), jnp.where(side == 0, mom_other, mom_mine)], 0
    )
    return (cells_now - mom, regions)


def solution(mesh):
    in_specs = (
        P("cell", "region"),
        P("cell", "region"),
        P(),
        P("cell", None),
        P(("cell", "region"), None),
    )
    out_specs = (P("cell", None), P(("cell", "region"), None))

    return jax.shard_map(body, mesh=mesh, in_specs=in_specs, out_specs=out_specs, check_vma=False)
```

time: 220 us -> 183 us (0.83)
  waiting for transfers between devices: 139 us -> 80.5 us
  Pallas kernels: 0 us -> 41.5 us
  matrix products: 32.3 us -> 0 us
  starting transfers between devices: 17.1 us -> 43.3 us
  between operations: 19.2 us -> 1.02 us
  local copies, waits for them, and re-layouts: 4.15 us -> 7.44 us
    psum x4 -> x0, waiting for transfers between devices: 133 us -> none  [body(): grad_total = lax.psum(grad_cell, 'region')]
    ppermute x4 -> x22, waiting for transfers between devices: 5.62 us -> 80.5 us  [the longest x21 59.5 us: permuted(): return lax.ppermute(value, axis, pairs)]
    pallas_call x0 -> x8, Pallas kernels: none -> 41.5 us  [block_call(): pl.pallas_call(functools.partial(block_kernel, (section, chunk, scale, ra...]
    dot_general x12 -> x0, matrix products: 32.3 us -> none  [the longest x4 13.6 us: body(): lax.dot_general(cell_bf, region_bf, (((1,), (1,)), ((), ())), preferred_e...]
    ppermute x4 -> x22, starting transfers between devices: 16.9 us -> 43.3 us  [the longest x21 38.8 us: permuted(): return lax.ppermute(value, axis, pairs)]
    sub x4 -> x1, other arithmetic: 7.45 us -> 1.11 us  [body(): return (cells_now - mom, regions)]
    unnamed x9 -> x41, local copies, waits for them, and re-layouts: 2.28 us -> 7.4 us
    add x0 -> x8, other arithmetic: none -> 4.82 us  [the longest x4 4.44 us: body(): grad_mine = grad_keep + permuted(grad_send, 'region', lambda i: i ^ bits[0])]
  transfers between devices with their start and end apart: 8 -> 22, of which waited for: 5 -> 13; matrix products, arithmetic and copies ran while one was open for 8% -> 1% of each run, Pallas kernels for 0% -> 9%
where the time goes in v1:
time: 183 us; the launch traced here: 182 us
  waiting for transfers between devices  80.5 us (44%)
  starting transfers between devices  43.3 us (24%)
  Pallas kernels  41.5 us (23%)
  other arithmetic  8.02 us (4%)
  local copies, waits for them, and re-layouts  7.44 us (4%)
    ppermute x21, waiting for transfers between devices, permuted(): return lax.ppermute(value, axis, pairs)  59.5 us
    pallas_call x8, Pallas kernels, block_call(): pl.pallas_call(functools.partial(block_kernel, (section, chunk, scale, ra...  41.5 us
    ppermute x21, starting transfers between devices, permuted(): return lax.ppermute(value, axis, pairs)  38.8 us
    ppermute x1, waiting for transfers between devices, returned(): lax.ppermute(relay, 'cell', [(i, (i + steps + 1) % count) for i in range(...  21.1 us
    unnamed x41, local copies, waits for them, and re-layouts  7.4 us
    ppermute x1, starting transfers between devices, returned(): lax.ppermute(relay, 'cell', [(i, (i + steps + 1) % count) for i in range(...  4.53 us
    add x4, other arithmetic, body(): grad_mine = grad_keep + permuted(grad_send, 'region', lambda i: i ^ bits[0])  4.44 us
  transfers between devices with their start and end apart: 22, of which 13 were waited for; matrix products, arithmetic and copies ran while one was open for 1% of the time, Pallas kernels for 9%

profile of v1, /device:TPU:0, one launch (start us, length us, event | category | flops | bytes accessed | tf_op | source)
XLA Modules:
  0.0 181.8 jit_solution(3560518389490874221)
XLA Ops:
  0.6 1.4 copy.13.mask
  2.1 5.1 %shard_map.68 = (f32[512,256]{1,0:T(8,128)}, bf16[1024,256]{1,0:T(8,128)(2,1)}, f32[1024,256]{1,0:T(8,128)}) custom-call(s32[4]{0:T(128)} %plan.15, bf16[1024,4096]{1,0:T(8,128)(2,1)} %observed.15, s32[128,32]{1,0:T(8,128)} %copy.13.mask, f32[1024,256]{1,0:T(8,128)} %refs_0_.3, f32[1024,256]{1,0:T(8,128)} %refs_2_.1), custom_call_target="tpu_custom_call" | custom-call | flops 805306368 | bytes 4194304 | tf_op jit(solution)/shard_map/pallas_call | solution.py:168
  7.2 5.3 %shard_map.69 = (f32[512,256]{1,0:T(8,128)}, f32[512,256]{1,0:T(8,128)}, f32[512,256]{1,0:T(8,128)}) custom-call(s32[4]{0:T(128)} %plan.15, bf16[1024,4096]{1,0:T(8,128)(2,1)} %observed.15, s32[128,32]{1,0:T(8,128)} %copy.13.mask, bf16[1024,256]{1,0:T(8,128)(2,1)} %get-tuple-element.29.refs_0_, f32[1024,256]{1,0:T(8,128)} %get-tuple-element.30.refs_1_, ...), custom_call_target="tpu_custom_call" | custom-call | flops 805306368 | bytes 4194304 | tf_op jit(solution)/shard_map/pallas_call | solution.py:168
  12.5 0.6 collective-permute-start
  13.1 1.7 collective-permute-done
  14.8 1.1 add.40
  16.0 2.9 %collective-permute-start.1 = (f32[512,256]{1,0:T(8,128)S(1)}, f32[512,256]{1,0:T(8,128)S(1)}, u32[]{:S(2)}, u32[]{:S(2)}) collective-permute-start(f32[512,256]{1,0:T(8,128)S(1)} %add.40), channel_id=1, source_target_pairs={{0,2},{1,3},{2,0},{3,1},{4,6},{5,7},{6,4},{7,5},{8,10},{9,11},{10,... | collective-permute-start | bytes 1572872 | tf_op jit(solution)/shard_map/ppermute | solution.py:24
  18.9 4.6 %collective-permute-start.3 = (f32[512,256]{1,0:T(8,128)S(1)}, f32[512,256]{1,0:T(8,128)S(1)}, u32[]{:S(2)}, u32[]{:S(2)}) collective-permute-start(f32[512,256]{1,0:T(8,128)S(1)} %copy-done.19), channel_id=1, source_target_pairs={{0,28},{4,0},{8,4},{12,8},{16,12},{20,16},{24,20},{28,24},{1,29},{... | collective-permute-start | bytes 1572872 | tf_op jit(solution)/shard_map/ppermute | solution.py:24
  23.4 7.7 %collective-permute-done.1 = f32[512,256]{1,0:T(8,128)S(1)} collective-permute-done((f32[512,256]{1,0:T(8,128)S(1)}, f32[512,256]{1,0:T(8,128)S(1)}, u32[]{:S(2)}, u32[]{:S(2)}) %collective-permute-start.1) | collective-permute-done | bytes 524320 | tf_op jit(solution)/shard_map/ppermute | solution.py:24
  31.1 0.1 add.41.refs_1_
  31.2 0.1 collective-permute-start.2
  31.3 4.9 %collective-permute-start.4 = (f32[512,256]{1,0:T(8,128)}, f32[512,256]{1,0:T(8,128)S(1)}, u32[]{:S(2)}, u32[]{:S(2)}) collective-permute-start(f32[512,256]{1,0:T(8,128)} %get-tuple-element.37), channel_id=1, source_target_pairs={{0,28},{4,0},{8,4},{12,8},{16,12},{20,16},{24,20},{28,24},{1,29},{... | collective-permute-start | bytes 1572872 | tf_op jit(solution)/shard_map/ppermute | solution.py:24
  36.1 0.8 copy-done.9
  36.9 0.8 copy-done.12
  37.7 5.3 %shard_map.70 = (f32[512,256]{1,0:T(8,128)}, f32[1024,256]{1,0:T(8,128)}, bf16[1024,256]{1,0:T(8,128)(2,1)}, f32[1024,256]{1,0:T(8,128)}) custom-call(s32[4]{0:T(128)} %plan.15, bf16[1024,4096]{1,0:T(8,128)(2,1)} %observed.15, s32[128,32]{1,0:T(8,128)} %copy.13.mask, f32[1024,256]{1,0:T(8,128)} %refs_0_.3, f32[512,256]{1,0:T(8,128)} %copy-done, ...), custom_call_target="tpu_custom_call" | custom-call | flops 805306368 | bytes 4194304 | tf_op jit(solution)/shard_map/pallas_call | solution.py:168
  43.0 5.2 %collective-permute-done.4.refs_2_ = f32[512,256]{1,0:T(8,128)S(1)} collective-permute-done((f32[512,256]{1,0:T(8,128)}, f32[512,256]{1,0:T(8,128)S(1)}, u32[]{:S(2)}, u32[]{:S(2)}) %collective-permute-start.4) | collective-permute-done | bytes 524320 | tf_op jit(solution)/shard_map/ppermute | solution.py:24
  48.2 0.8 copy-done.16
  49.1 5.0 %shard_map.71 = (f32[512,256]{1,0:T(8,128)}, f32[512,256]{1,0:T(8,128)}, f32[512,256]{1,0:T(8,128)}) custom-call(s32[4]{0:T(128)} %plan.15, bf16[1024,4096]{1,0:T(8,128)(2,1)} %observed.15, s32[128,32]{1,0:T(8,128)} %copy.13.mask, bf16[1024,256]{1,0:T(8,128)(2,1)} %get-tuple-element.35.refs_0_, f32[1024,256]{1,0:T(8,128)} %get-tuple-element.36.refs_1_, ...), custom_call_target="tpu_custom_call" | custom-call | flops 805306368 | bytes 4194304 | tf_op jit(solution)/shard_map/pallas_call | solution.py:168
  54.1 0.1 collective-permute-start.5
  54.2 2.1 %collective-permute-done.5 = f32[512,256]{1,0:T(8,128)S(1)} collective-permute-done((f32[512,256]{1,0:T(8,128)}, f32[512,256]{1,0:T(8,128)S(1)}, u32[]{:S(2)}, u32[]{:S(2)}) %collective-permute-start.5) | collective-permute-done | bytes 524320 | tf_op jit(solution)/shard_map/ppermute | solution.py:24
  56.3 1.1 add.42
  57.4 1.6 collective-permute-start.6
  58.9 5.1 %collective-permute-start.8 = (f32[512,256]{1,0:T(8,128)S(1)}, f32[512,256]{1,0:T(8,128)S(1)}, u32[]{:S(2)}, u32[]{:S(2)}) collective-permute-start(f32[512,256]{1,0:T(8,128)S(1)} %copy-done.18), channel_id=1, source_target_pairs={{0,28},{4,0},{8,4},{12,8},{16,12},{20,16},{24,20},{28,24},{1,29},{... | collective-permute-start | bytes 1572872 | tf_op jit(solution)/shard_map/ppermute | solution.py:24
  64.0 7.4 %collective-permute-done.6 = f32[512,256]{1,0:T(8,128)S(1)} collective-permute-done((f32[512,256]{1,0:T(8,128)S(1)}, f32[512,256]{1,0:T(8,128)S(1)}, u32[]{:S(2)}, u32[]{:S(2)}) %collective-permute-start.6) | collective-permute-done | bytes 524320 | tf_op jit(solution)/shard_map/ppermute | solution.py:24
  71.4 0.1 add_add_fusion.2.refs_1_
  71.5 0.1 collective-permute-start.7
  71.6 5.1 %collective-permute-start.9 = (f32[512,256]{1,0:T(8,128)}, f32[512,256]{1,0:T(8,128)S(1)}, u32[]{:S(2)}, u32[]{:S(2)}) collective-permute-start(f32[512,256]{1,0:T(8,128)} %get-tuple-element.44), channel_id=1, source_target_pairs={{0,28},{4,0},{8,4},{12,8},{16,12},{20,16},{24,20},{28,24},{1,29},{... | collective-permute-start | bytes 1572872 | tf_op jit(solution)/shard_map/ppermute | solution.py:24
  76.8 0.8 copy-done.7
  77.5 0.2 copy-done.10
  77.7 5.3 %shard_map.72 = (f32[512,256]{1,0:T(8,128)}, f32[1024,256]{1,0:T(8,128)}, bf16[1024,256]{1,0:T(8,128)(2,1)}, f32[1024,256]{1,0:T(8,128)}) custom-call(s32[4]{0:T(128)} %plan.15, bf16[1024,4096]{1,0:T(8,128)(2,1)} %observed.15, s32[128,32]{1,0:T(8,128)} %copy.13.mask, f32[1024,256]{1,0:T(8,128)} %get-tuple-element.34.refs_0_, f32[512,256]{1,0:T(8,128)} %copy-done.4, ...), custom_call_target="tpu_custom_call" | custom-call | flops 805306368 | bytes 4194304 | tf_op jit(solution)/shard_map/pallas_call | solution.py:168
  83.0 5.8 %collective-permute-done.9.refs_2_ = f32[512,256]{1,0:T(8,128)S(1)} collective-permute-done((f32[512,256]{1,0:T(8,128)}, f32[512,256]{1,0:T(8,128)S(1)}, u32[]{:S(2)}, u32[]{:S(2)}) %collective-permute-start.9) | collective-permute-done | bytes 524320 | tf_op jit(solution)/shard_map/ppermute | solution.py:24
  88.9 0.8 copy-done.15
  89.6 5.0 %shard_map.73 = (f32[512,256]{1,0:T(8,128)}, f32[512,256]{1,0:T(8,128)}, f32[512,256]{1,0:T(8,128)}) custom-call(s32[4]{0:T(128)} %plan.15, bf16[1024,4096]{1,0:T(8,128)(2,1)} %observed.15, s32[128,32]{1,0:T(8,128)} %copy.13.mask, bf16[1024,256]{1,0:T(8,128)(2,1)} %get-tuple-element.42.refs_0_, f32[1024,256]{1,0:T(8,128)} %get-tuple-element.43.refs_1_, ...), custom_call_target="tpu_custom_call" | custom-call | flops 805306368 | bytes 4194304 | tf_op jit(solution)/shard_map/pallas_call | solution.py:168
  94.7 0.1 collective-permute-start.10
  94.8 2.1 %collective-permute-done.10 = f32[512,256]{1,0:T(8,128)S(1)} collective-permute-done((f32[512,256]{1,0:T(8,128)}, f32[512,256]{1,0:T(8,128)S(1)}, u32[]{:S(2)}, u32[]{:S(2)}) %collective-permute-start.10) | collective-permute-done | bytes 524320 | tf_op jit(solution)/shard_map/ppermute | solution.py:24
  96.9 1.1 add.45
  98.0 1.6 collective-permute-start.11
  99.5 5.1 %collective-permute-start.13 = (f32[512,256]{1,0:T(8,128)S(1)}, f32[512,256]{1,0:T(8,128)S(1)}, u32[]{:S(2)}, u32[]{:S(2)}) collective-permute-start(f32[512,256]{1,0:T(8,128)S(1)} %copy-done.17), channel_id=1, source_target_pairs={{0,28},{4,0},{8,4},{12,8},{16,12},{20,16},{24,20},{28,24},{1,29},{... | collective-permute-start | bytes 1572872 | tf_op jit(solution)/shard_map/ppermute | solution.py:24
  104.6 7.4 %collective-permute-done.11 = f32[512,256]{1,0:T(8,128)S(1)} collective-permute-done((f32[512,256]{1,0:T(8,128)S(1)}, f32[512,256]{1,0:T(8,128)S(1)}, u32[]{:S(2)}, u32[]{:S(2)}) %collective-permute-start.11) | collective-permute-done | bytes 524320 | tf_op jit(solution)/shard_map/ppermute | solution.py:24
  112.0 0.1 add_add_fusion.1.refs_1_
  112.1 0.1 collective-permute-start.12
  112.2 5.3 %collective-permute-start.14 = (f32[512,256]{1,0:T(8,128)}, f32[512,256]{1,0:T(8,128)S(1)}, u32[]{:S(2)}, u32[]{:S(2)}) collective-permute-start(f32[512,256]{1,0:T(8,128)} %get-tuple-element.51), channel_id=1, source_target_pairs={{0,28},{4,0},{8,4},{12,8},{16,12},{20,16},{24,20},{28,24},{1,29},{... | collective-permute-start | bytes 1572872 | tf_op jit(solution)/shard_map/ppermute | solution.py:24
  117.6 0.8 copy-done.8
  118.3 0.2 copy-done.11
  118.5 5.3 %shard_map.74 = (f32[512,256]{1,0:T(8,128)}, f32[1024,256]{1,0:T(8,128)}, bf16[1024,256]{1,0:T(8,128)(2,1)}, f32[1024,256]{1,0:T(8,128)}) custom-call(s32[4]{0:T(128)} %plan.15, bf16[1024,4096]{1,0:T(8,128)(2,1)} %observed.15, s32[128,32]{1,0:T(8,128)} %copy.13.mask, f32[1024,256]{1,0:T(8,128)} %get-tuple-element.41.refs_0_, f32[512,256]{1,0:T(8,128)} %copy-done.2, ...), custom_call_target="tpu_custom_call" | custom-call | flops 805306368 | bytes 4194304 | tf_op jit(solution)/shard_map/pallas_call | solution.py:168
  123.8 5.6 %collective-permute-done.14.refs_2_ = f32[512,256]{1,0:T(8,128)S(1)} collective-permute-done((f32[512,256]{1,0:T(8,128)}, f32[512,256]{1,0:T(8,128)S(1)}, u32[]{:S(2)}, u32[]{:S(2)}) %collective-permute-start.14) | collective-permute-done | bytes 524320 | tf_op jit(solution)/shard_map/ppermute | solution.py:24
  129.4 0.8 copy-done.14
  130.2 5.1 %shard_map.75 = (f32[512,256]{1,0:T(8,128)}, f32[512,256]{1,0:T(8,128)}, f32[512,256]{1,0:T(8,128)}) custom-call(s32[4]{0:T(128)} %plan.15, bf16[1024,4096]{1,0:T(8,128)(2,1)} %observed.15, s32[128,32]{1,0:T(8,128)} %copy.13.mask, bf16[1024,256]{1,0:T(8,128)(2,1)} %get-tuple-element.49.refs_0_, f32[1024,256]{1,0:T(8,128)} %get-tuple-element.50.refs_1_, ...), custom_call_target="tpu_custom_call" | custom-call | flops 805306368 | bytes 4194304 | tf_op jit(solution)/shard_map/pallas_call | solution.py:168
  135.4 0.1 collective-permute-start.15
  135.4 2.1 %collective-permute-done.15 = f32[512,256]{1,0:T(8,128)S(1)} collective-permute-done((f32[512,256]{1,0:T(8,128)}, f32[512,256]{1,0:T(8,128)S(1)}, u32[]{:S(2)}, u32[]{:S(2)}) %collective-permute-start.15) | collective-permute-done | bytes 524320 | tf_op jit(solution)/shard_map/ppermute | solution.py:24
  137.5 1.1 add.49
  138.7 1.6 collective-permute-start.16
  140.3 0.1 collective-permute-start.18
  140.3 0.1 collective-permute-start.21
  140.4 9.6 %collective-permute-done.18 = f32[256,256]{1,0:T(8,128)S(1)} collective-permute-done((f32[256,256]{1,0:T(8,128)S(1)}, f32[256,256]{1,0:T(8,128)S(1)}, u32[]{:S(2)}, u32[]{:S(2)}) %collective-permute-start.18) | collective-permute-done | bytes 262176 | tf_op jit(solution)/shard_map/ppermute | solution.py:24
  150.0 4.5 %collective-permute-start.19 = (f32[256,256]{1,0:T(8,128)S(1)}, f32[256,256]{1,0:T(8,128)S(1)}, u32[]{:S(2)}, u32[]{:S(2)}) collective-permute-start(f32[256,256]{1,0:T(8,128)S(1)} %collective-permute-done.18), channel_id=1, source_target_pairs={{0,16},{8,24},{16,0},{24,8},{1,17},{9,25},{17,1},{25,9},{2,18},{10... | collective-permute-start | bytes 786440 | tf_op jit(solution)/shard_map/ppermute | solution.py:211
  154.6 0.1 add_add_fusion
  154.7 0.1 collective-permute-start.17
  154.8 0.1 collective-permute-start.20
  154.8 21.1 %collective-permute-done.19 = f32[256,256]{1,0:T(8,128)S(1)} collective-permute-done((f32[256,256]{1,0:T(8,128)S(1)}, f32[256,256]{1,0:T(8,128)S(1)}, u32[]{:S(2)}, u32[]{:S(2)}) %collective-permute-start.19) | collective-permute-done | bytes 262176 | tf_op jit(solution)/shard_map/ppermute | solution.py:211
  176.0 2.7 %collective-permute-done.20 = f32[256,256]{1,0:T(8,128)} collective-permute-done((f32[256,256]{1,0:T(8,128)S(1)}, f32[256,256]{1,0:T(8,128)}, u32[]{:S(2)}, u32[]{:S(2)}) %collective-permute-start.20) | collective-permute-done | bytes 262176 | tf_op jit(solution)/shard_map/ppermute | solution.py:24
  178.6 2.0 %pad_maximum_fusion = f32[1024,256]{1,0:T(8,128)} fusion(f32[512,256]{1,0:T(8,128)S(1)} %collective-permute-done.21, f32[256,256]{1,0:T(8,128)} %collective-permute-done.20, f32[256,256]{1,0:T(8,128)S(1)} %broadcast_select_fusion.2), kind=kLoop, calls=%fused_computation.1 | loop fusion | flops 524288 | bytes 2097152 | tf_op jit(solution)/shard_map/concatenate | solution.py:212
  180.6 0.1 broadcast_select_fusion.1
  180.7 1.1 maximum_subtract_fusion
  (42 shorter events, 0.2 us)
Async XLA Ops:
  7.2 11.7 %copy-start.19 = (f32[512,256]{1,0:T(8,128)S(1)}, f32[512,256]{1,0:T(8,128)}, u32[]{:S(2)}) copy-start(f32[512,256]{1,0:T(8,128)} %get-tuple-element.33) | copy-start | bytes 1572868
  12.5 2.3 %collective-permute-start = (f32[512,256]{1,0:T(8,128)}, f32[512,256]{1,0:T(8,128)S(1)}, u32[]{:S(2)}, u32[]{:S(2)}) collective-permute-start(f32[512,256]{1,0:T(8,128)} %get-tuple-element.32), channel_id=1, source_target_pairs={{0,1},{1,0},{2,3},{3,2},{4,5},{5,4},{6,7},{7,6},{8,9},{9,8},{10,11... | collective-permute-start | bytes 1572872 | tf_op jit(solution)/shard_map/ppermute | solution.py:24
  16.0 15.1 %collective-permute-start.1 = (f32[512,256]{1,0:T(8,128)S(1)}, f32[512,256]{1,0:T(8,128)S(1)}, u32[]{:S(2)}, u32[]{:S(2)}) collective-permute-start(f32[512,256]{1,0:T(8,128)S(1)} %add.40), channel_id=1, source_target_pairs={{0,2},{1,3},{2,0},{3,1},{4,6},{5,7},{6,4},{7,5},{8,10},{9,11},{10,... | collective-permute-start | bytes 1572872 | tf_op jit(solution)/shard_map/ppermute | solution.py:24
  18.9 17.3 %collective-permute-start.3 = (f32[512,256]{1,0:T(8,128)S(1)}, f32[512,256]{1,0:T(8,128)S(1)}, u32[]{:S(2)}, u32[]{:S(2)}) collective-permute-start(f32[512,256]{1,0:T(8,128)S(1)} %copy-done.19), channel_id=1, source_target_pairs={{0,28},{4,0},{8,4},{12,8},{16,12},{20,16},{24,20},{28,24},{1,29},{... | collective-permute-start | bytes 1572872 | tf_op jit(solution)/shard_map/ppermute | solution.py:24
  31.2 5.0 %copy-start = (f32[512,256]{1,0:T(8,128)}, f32[512,256]{1,0:T(8,128)S(1)}, u32[]{:S(2)}) copy-start(f32[512,256]{1,0:T(8,128)S(1)} %add.41.refs_1_) | copy-start | bytes 1572868
  31.2 5.0 %collective-permute-start.2 = (f32[512,256]{1,0:T(8,128)S(1)}, f32[512,256]{1,0:T(8,128)S(1)}, u32[]{:S(2)}, u32[]{:S(2)}) collective-permute-start(f32[512,256]{1,0:T(8,128)S(1)} %add.41.refs_1_), channel_id=1, source_target_pairs={{0,1},{1,0},{2,3},{3,2},{4,5},{5,4},{6,7},{7,6},{8,9},{9,8},{10,11... | collective-permute-start | bytes 1572872 | tf_op jit(solution)/shard_map/ppermute | solution.py:24
  31.3 17.0 %collective-permute-start.4 = (f32[512,256]{1,0:T(8,128)}, f32[512,256]{1,0:T(8,128)S(1)}, u32[]{:S(2)}, u32[]{:S(2)}) collective-permute-start(f32[512,256]{1,0:T(8,128)} %get-tuple-element.37), channel_id=1, source_target_pairs={{0,28},{4,0},{8,4},{12,8},{16,12},{20,16},{24,20},{28,24},{1,29},{... | collective-permute-start | bytes 1572872 | tf_op jit(solution)/shard_map/ppermute | solution.py:24
  36.1 0.8 copy-start.9
  36.9 0.8 copy-start.12
  43.0 15.9 %copy-start.18 = (f32[512,256]{1,0:T(8,128)S(1)}, f32[512,256]{1,0:T(8,128)}, u32[]{:S(2)}) copy-start(f32[512,256]{1,0:T(8,128)} %get-tuple-element.40) | copy-start | bytes 1572868
  43.0 28.4 %copy-start.1 = (f32[512,256]{1,0:T(8,128)S(1)}, f32[512,256]{1,0:T(8,128)}, u32[]{:S(2)}) copy-start(f32[512,256]{1,0:T(8,128)} %copy-done) | copy-start | bytes 1572868
  48.2 0.8 copy-start.16
  54.1 2.2 %collective-permute-start.5 = (f32[512,256]{1,0:T(8,128)}, f32[512,256]{1,0:T(8,128)S(1)}, u32[]{:S(2)}, u32[]{:S(2)}) collective-permute-start(f32[512,256]{1,0:T(8,128)} %get-tuple-element.39), channel_id=1, source_target_pairs={{0,1},{1,0},{2,3},{3,2},{4,5},{5,4},{6,7},{7,6},{8,9},{9,8},{10,11... | collective-permute-start | bytes 1572872 | tf_op jit(solution)/shard_map/ppermute | solution.py:24
  57.4 14.0 %collective-permute-start.6 = (f32[512,256]{1,0:T(8,128)S(1)}, f32[512,256]{1,0:T(8,128)S(1)}, u32[]{:S(2)}, u32[]{:S(2)}) collective-permute-start(f32[512,256]{1,0:T(8,128)S(1)} %add.42), channel_id=1, source_target_pairs={{0,2},{1,3},{2,0},{3,1},{4,6},{5,7},{6,4},{7,5},{8,10},{9,11},{10,... | collective-permute-start | bytes 1572872 | tf_op jit(solution)/shard_map/ppermute | solution.py:24
  58.9 17.8 %collective-permute-start.8 = (f32[512,256]{1,0:T(8,128)S(1)}, f32[512,256]{1,0:T(8,128)S(1)}, u32[]{:S(2)}, u32[]{:S(2)}) collective-permute-start(f32[512,256]{1,0:T(8,128)S(1)} %copy-done.18), channel_id=1, source_target_pairs={{0,28},{4,0},{8,4},{12,8},{16,12},{20,16},{24,20},{28,24},{1,29},{... | collective-permute-start | bytes 1572872 | tf_op jit(solution)/shard_map/ppermute | solution.py:24
  71.5 5.2 %copy-start.4 = (f32[512,256]{1,0:T(8,128)}, f32[512,256]{1,0:T(8,128)S(1)}, u32[]{:S(2)}) copy-start(f32[512,256]{1,0:T(8,128)S(1)} %add_add_fusion.2.refs_1_) | copy-start | bytes 1572868
  71.5 5.2 %collective-permute-start.7 = (f32[512,256]{1,0:T(8,128)S(1)}, f32[512,256]{1,0:T(8,128)S(1)}, u32[]{:S(2)}, u32[]{:S(2)}) collective-permute-start(f32[512,256]{1,0:T(8,128)S(1)} %add_add_fusion.2.refs_1_), channel_id=1, source_target_pairs={{0,1},{1,0},{2,3},{3,2},{4,5},{5,4},{6,7},{7,6},{8,9},{9,8},{10,11... | collective-permute-start | bytes 1572872 | tf_op jit(solution)/shard_map/ppermute | solution.py:24
  71.6 17.2 %collective-permute-start.9 = (f32[512,256]{1,0:T(8,128)}, f32[512,256]{1,0:T(8,128)S(1)}, u32[]{:S(2)}, u32[]{:S(2)}) collective-permute-start(f32[512,256]{1,0:T(8,128)} %get-tuple-element.44), channel_id=1, source_target_pairs={{0,28},{4,0},{8,4},{12,8},{16,12},{20,16},{24,20},{28,24},{1,29},{... | collective-permute-start | bytes 1572872 | tf_op jit(solution)/shard_map/ppermute | solution.py:24
  76.7 0.8 copy-start.7
  76.8 1.0 copy-start.10
  83.0 16.5 %copy-start.17 = (f32[512,256]{1,0:T(8,128)S(1)}, f32[512,256]{1,0:T(8,128)}, u32[]{:S(2)}) copy-start(f32[512,256]{1,0:T(8,128)} %get-tuple-element.47) | copy-start | bytes 1572868
  83.0 29.0 %copy-start.5 = (f32[512,256]{1,0:T(8,128)S(1)}, f32[512,256]{1,0:T(8,128)}, u32[]{:S(2)}) copy-start(f32[512,256]{1,0:T(8,128)} %copy-done.4) | copy-start | bytes 1572868
  88.9 0.8 copy-start.15
  94.7 2.2 %collective-permute-start.10 = (f32[512,256]{1,0:T(8,128)}, f32[512,256]{1,0:T(8,128)S(1)}, u32[]{:S(2)}, u32[]{:S(2)}) collective-permute-start(f32[512,256]{1,0:T(8,128)} %get-tuple-element.46), channel_id=1, source_target_pairs={{0,1},{1,0},{2,3},{3,2},{4,5},{5,4},{6,7},{7,6},{8,9},{9,8},{10,11... | collective-permute-start | bytes 1572872 | tf_op jit(solution)/shard_map/ppermute | solution.py:24
  98.0 14.0 %collective-permute-start.11 = (f32[512,256]{1,0:T(8,128)S(1)}, f32[512,256]{1,0:T(8,128)S(1)}, u32[]{:S(2)}, u32[]{:S(2)}) collective-permute-start(f32[512,256]{1,0:T(8,128)S(1)} %add.45), channel_id=1, source_target_pairs={{0,2},{1,3},{2,0},{3,1},{4,6},{5,7},{6,4},{7,5},{8,10},{9,11},{10,... | collective-permute-start | bytes 1572872 | tf_op jit(solution)/shard_map/ppermute | solution.py:24
  99.5 18.0 %collective-permute-start.13 = (f32[512,256]{1,0:T(8,128)S(1)}, f32[512,256]{1,0:T(8,128)S(1)}, u32[]{:S(2)}, u32[]{:S(2)}) collective-permute-start(f32[512,256]{1,0:T(8,128)S(1)} %copy-done.17), channel_id=1, source_target_pairs={{0,28},{4,0},{8,4},{12,8},{16,12},{20,16},{24,20},{28,24},{1,29},{... | collective-permute-start | bytes 1572872 | tf_op jit(solution)/shard_map/ppermute | solution.py:24
  112.1 5.4 %copy-start.2 = (f32[512,256]{1,0:T(8,128)}, f32[512,256]{1,0:T(8,128)S(1)}, u32[]{:S(2)}) copy-start(f32[512,256]{1,0:T(8,128)S(1)} %add_add_fusion.1.refs_1_) | copy-start | bytes 1572868
  112.1 5.4 %collective-permute-start.12 = (f32[512,256]{1,0:T(8,128)S(1)}, f32[512,256]{1,0:T(8,128)S(1)}, u32[]{:S(2)}, u32[]{:S(2)}) collective-permute-start(f32[512,256]{1,0:T(8,128)S(1)} %add_add_fusion.1.refs_1_), channel_id=1, source_target_pairs={{0,1},{1,0},{2,3},{3,2},{4,5},{5,4},{6,7},{7,6},{8,9},{9,8},{10,11... | collective-permute-start | bytes 1572872 | tf_op jit(solution)/shard_map/ppermute | solution.py:24
  112.2 17.2 %collective-permute-start.14 = (f32[512,256]{1,0:T(8,128)}, f32[512,256]{1,0:T(8,128)S(1)}, u32[]{:S(2)}, u32[]{:S(2)}) collective-permute-start(f32[512,256]{1,0:T(8,128)} %get-tuple-element.51), channel_id=1, source_target_pairs={{0,28},{4,0},{8,4},{12,8},{16,12},{20,16},{24,20},{28,24},{1,29},{... | collective-permute-start | bytes 1572872 | tf_op jit(solution)/shard_map/ppermute | solution.py:24
  117.5 0.8 copy-start.8
  117.5 1.0 copy-start.11
  123.8 16.4 %copy-start.13 = (f32[512,256]{1,0:T(8,128)S(1)}, f32[512,256]{1,0:T(8,128)}, u32[]{:S(2)}) copy-start(f32[512,256]{1,0:T(8,128)} %get-tuple-element.54) | copy-start | bytes 1572868
  123.8 30.8 %copy-start.3 = (f32[512,256]{1,0:T(8,128)S(1)}, f32[512,256]{1,0:T(8,128)}, u32[]{:S(2)}) copy-start(f32[512,256]{1,0:T(8,128)} %copy-done.2) | copy-start | bytes 1572868
  129.4 0.8 copy-start.14
  130.2 50.5 %copy-start.6 = (f32[1024,256]{1,0:T(8,128)S(1)}, f32[1024,256]{1,0:T(8,128)}, u32[]{:S(2)}) copy-start(f32[1024,256]{1,0:T(8,128)} %get-tuple-element.48) | copy-start | bytes 3145732
  135.4 2.2 %collective-permute-start.15 = (f32[512,256]{1,0:T(8,128)}, f32[512,256]{1,0:T(8,128)S(1)}, u32[]{:S(2)}, u32[]{:S(2)}) collective-permute-start(f32[512,256]{1,0:T(8,128)} %get-tuple-element.53), channel_id=1, source_target_pairs={{0,1},{1,0},{2,3},{3,2},{4,5},{5,4},{6,7},{7,6},{8,9},{9,8},{10,11... | collective-permute-start | bytes 1572872 | tf_op jit(solution)/shard_map/ppermute | solution.py:24
  138.7 15.9 %collective-permute-start.16 = (f32[512,256]{1,0:T(8,128)S(1)}, f32[512,256]{1,0:T(8,128)S(1)}, u32[]{:S(2)}, u32[]{:S(2)}) collective-permute-start(f32[512,256]{1,0:T(8,128)S(1)} %add.49), channel_id=1, source_target_pairs={{0,2},{1,3},{2,0},{3,1},{4,6},{5,7},{6,4},{7,5},{8,10},{9,11},{10,... | collective-permute-start | bytes 1572872 | tf_op jit(solution)/shard_map/ppermute | solution.py:24
  140.3 9.8 %collective-permute-start.18 = (f32[256,256]{1,0:T(8,128)S(1)}, f32[256,256]{1,0:T(8,128)S(1)}, u32[]{:S(2)}, u32[]{:S(2)}) collective-permute-start(f32[256,256]{1,0:T(8,128)S(1)} %get-tuple-element.58), channel_id=1, source_target_pairs={{0,12},{4,0},{8,20},{12,8},{16,28},{20,16},{24,4},{28,24},{1,13},{... | collective-permute-start | bytes 786440 | tf_op jit(solution)/shard_map/ppermute | solution.py:24
  140.3 38.3 %collective-permute-start.21 = (f32[512,256]{1,0:T(8,128)}, f32[512,256]{1,0:T(8,128)S(1)}, u32[]{:S(2)}, u32[]{:S(2)}) collective-permute-start(f32[512,256]{1,0:T(8,128)} %get-tuple-element.55), channel_id=1, source_target_pairs={{0,12},{4,16},{8,20},{12,24},{16,28},{20,0},{24,4},{28,8},{1,13},{... | collective-permute-start | bytes 1572872 | tf_op jit(solution)/shard_map/ppermute | solution.py:24
  150.0 25.9 %collective-permute-start.19 = (f32[256,256]{1,0:T(8,128)S(1)}, f32[256,256]{1,0:T(8,128)S(1)}, u32[]{:S(2)}, u32[]{:S(2)}) collective-permute-start(f32[256,256]{1,0:T(8,128)S(1)} %collective-permute-done.18), channel_id=1, source_target_pairs={{0,16},{8,24},{16,0},{24,8},{1,17},{9,25},{17,1},{25,9},{2,18},{10... | collective-permute-start | bytes 786440 | tf_op jit(solution)/shard_map/ppermute | solution.py:211
  154.7 26.0 %collective-permute-start.17 = (f32[512,256]{1,0:T(8,128)S(1)}, f32[512,256]{1,0:T(8,128)S(1)}, u32[]{:S(2)}, u32[]{:S(2)}) collective-permute-start(f32[512,256]{1,0:T(8,128)S(1)} %add_add_fusion), channel_id=1, source_target_pairs={{0,1},{1,0},{2,3},{3,2},{4,5},{5,4},{6,7},{7,6},{8,9},{9,8},{10,11... | collective-permute-start | bytes 1572872 | tf_op jit(solution)/shard_map/ppermute | solution.py:24
  154.8 23.9 %collective-permute-start.20 = (f32[256,256]{1,0:T(8,128)S(1)}, f32[256,256]{1,0:T(8,128)}, u32[]{:S(2)}, u32[]{:S(2)}) collective-permute-start(f32[256,256]{1,0:T(8,128)S(1)} %get-tuple-element.59), channel_id=1, source_target_pairs={{0,12},{4,16},{8,20},{12,24},{16,28},{20,0},{24,4},{28,8},{1,13},{... | collective-permute-start | bytes 786440 | tf_op jit(solution)/shard_map/ppermute | solution.py:24
